TPU v7x, 32 devices: a whole 2x2x4 slice. The times are simulated.
32 devices in a mesh: seq: 8 (over z, x), head: 4 (over y, core).
Axes of the slice: x: 2, y: 2, z: 4, core: 2. Of those that a mesh axis runs over, the one named last changes fastest.
Arguments:
- queries: bfloat16 [1024, 4096], P('seq', 'head'), may hold values from -6 to 6
- keys: bfloat16 [1024, 4096], P('seq', 'head'), may hold values from -6 to 6
- values: bfloat16 [1024, 4096], P('seq', 'head'), may hold values from -3 to 3
- decay_codes: int32 [1024, 32], P('seq', 'head'), may hold values from 0 to 2048
- out_weight: bfloat16 [4096, 3072], P('head'), may hold values from -0.09375 to 0.09375
- out_grad: bfloat16 [1024, 3072], P('seq', 'head'), may hold values from -6 to 6
Outputs:
- mixed: bfloat16 [1024, 3072], P('seq', 'head')
- query_gradient: bfloat16 [1024, 4096], P('seq', 'head')
- key_grad: bfloat16 [1024, 4096], P('seq', 'head')
- value_gradient: bfloat16 [1024, 4096], P('seq', 'head')
All inputs are finite; a program needn't handle non-finite values.
Results may differ from a plain program's by a relative error of at most 0.014.
Values may be sent and summed in bfloat16 or wider, within the bound.
No kernel may reach another device: no remote copies, remote signals or barrier semaphores. Data moves between devices by JAX's collectives and lax.ppermute only.
A program may use at most 128 MiB of HBM per device.

v0:
```python
import jax
import jax.numpy as jnp
from jax import lax
from jax.sharding import PartitionSpec as P


def prefix(value, axis, join, neutral):
    count, mine = (lax.axis_size(axis), lax.axis_index(axis))
    pieces = jax.tree.map(lambda part: lax.all_gather(part, axis), value)
    subtotal = jax.tree.map(
        lambda part, zero: jnp.full_like(part, 0) + jnp.asarray(zero, part.dtype), value, neutral
    )

    def prefix_step(position, subtotal):
        longer = join(subtotal, jax.tree.map(lambda part: part[position], pieces))
        return jax.tree.map(lambda new, old: jnp.where(position < mine, new, old), longer, subtotal)

    return lax.fori_loop(0, count - 1, prefix_step, subtotal)


def entering(array, axis, combine, identity):
    devices, place = (lax.axis_size(axis), lax.axis_index(axis))
    everything = jax.tree.map(
        lambda part, kind: lax.all_gather(part.astype(kind), axis),
        array,
        (jnp.bfloat16, jnp.bfloat16),
    )
    start = jax.tree.map(
        lambda part, zero: jnp.broadcast_to(jnp.asarray(zero, part.dtype), part.shape),
        array,
        identity,
    )

    def entering_step(k, before):
        at = devices - 1 - k
        reached = at > place
        new = combine(
            before, jax.tree.map(lambda part, own: part[at].astype(own.dtype), everything, array)
        )
        return jax.tree.map(lambda a, b: jnp.where(reached, a, b), new, before)

    return lax.fori_loop(0, devices, entering_step, start)


def block_mask(cum_log):
    block_len = cum_log.shape[0]
    log_gap = cum_log.T[:, :, None] - cum_log.T[:, None, :]
    lower_part = (jnp.arange(block_len)[:, None] >= jnp.arange(block_len)[None, :])[None]
    return jnp.where(lower_part, jnp.exp(jnp.where(lower_part, log_gap, 0.0)), 0.0)


def combine(earlier, later):
    return (earlier[0] * later[0], later[0][:, None, None] * earlier[1] + later[1])


def local(queries, keys, values, decay_codes, out_weight, out_grad):
    tok_rows = queries.shape[0]
    head_count = decay_codes.shape[1]
    head_width = queries.shape[1] // head_count
    att_scale = 1.0 / head_width
    grad_flat = lax.dot_general(
        lax.all_gather(out_grad, "head", axis=1, tiled=True),
        out_weight,
        (((1,), (1,)), ((), ())),
        preferred_element_type=jnp.float32,
    ).astype(jnp.bfloat16)

    def to_heads(array):
        return array.reshape(tok_rows, head_count, head_width)

    query_h = to_heads(queries)
    key_h = to_heads(keys)
    value_h = to_heads(values)
    grad_h = to_heads(grad_flat)
    cum_log = jnp.cumsum(jnp.log(1.0 - decay_codes.astype(jnp.float32) / 4096.0), axis=0)
    decay_mask = block_mask(cum_log)
    rise_decay = jnp.exp(cum_log)[:, :, None]
    fall_decay = jnp.exp(cum_log[-1][None, :] - cum_log)[:, :, None]
    total_decay = jnp.exp(cum_log[-1])
    k_fall = (fall_decay * key_h.astype(jnp.float32)).astype(jnp.bfloat16)
    summary_fwd = jnp.einsum("thd,the->hde", k_fall, value_h, preferred_element_type=jnp.float32)
    q_rise = (att_scale * rise_decay * query_h.astype(jnp.float32)).astype(jnp.bfloat16)
    summary_bwd = jnp.einsum("shd,she->hde", q_rise, grad_h, preferred_element_type=jnp.float32)
    identity = (
        jnp.ones((head_count,), jnp.float32),
        jnp.zeros((head_count, head_width, head_width), jnp.float32),
    )
    passed_fwd, state_in = prefix((total_decay, summary_fwd), "seq", combine, identity)
    passed_bwd, carry_in = entering((total_decay, summary_bwd), "seq", combine, identity)
    scores = jnp.einsum("she,the->hst", query_h, key_h, preferred_element_type=jnp.float32)
    attn = (att_scale * scores * decay_mask).astype(jnp.bfloat16)
    pscores = jnp.einsum("she,the->hst", grad_h, value_h, preferred_element_type=jnp.float32)
    pmat = (att_scale * pscores * decay_mask).astype(jnp.bfloat16)
    g_rise = (att_scale * rise_decay * grad_h.astype(jnp.float32)).astype(jnp.bfloat16)
    v_fall = (fall_decay * value_h.astype(jnp.float32)).astype(jnp.bfloat16)
    local_out = jnp.einsum("hst,the->she", attn, value_h, preferred_element_type=jnp.float32)
    local_qgrad = jnp.einsum("hst,thd->shd", pmat, key_h, preferred_element_type=jnp.float32)
    local_kgrad = jnp.einsum("hst,shd->thd", pmat, query_h, preferred_element_type=jnp.float32)
    local_vgrad = jnp.einsum("hst,she->the", attn, grad_h, preferred_element_type=jnp.float32)
    state_b = state_in.astype(jnp.bfloat16)
    carry_b = carry_in.astype(jnp.bfloat16)
    attn_out = local_out + jnp.einsum(
        "shd,hde->she", q_rise, state_b, preferred_element_type=jnp.float32
    )
    query_gradient = local_qgrad + jnp.einsum(
        "she,hde->shd", g_rise, state_b, preferred_element_type=jnp.float32
    )
    key_grad = local_kgrad + jnp.einsum(
        "the,hde->thd", v_fall, carry_b, preferred_element_type=jnp.float32
    )
    value_gradient = local_vgrad + jnp.einsum(
        "thd,hde->the", k_fall, carry_b, preferred_element_type=jnp.float32
    )
    attn_flat = attn_out.astype(jnp.bfloat16).reshape(tok_rows, -1)
    partial_out = jnp.dot(attn_flat, out_weight, preferred_element_type=jnp.float32)
    mixed = lax.psum_scatter(
        partial_out.astype(jnp.bfloat16), "head", scatter_dimension=1, tiled=True
    )
    flat_width = queries.shape[1]
    return (
        mixed,
        query_gradient.astype(jnp.bfloat16).reshape(tok_rows, flat_width),
        key_grad.astype(jnp.bfloat16).reshape(tok_rows, flat_width),
        value_gradient.astype(jnp.bfloat16).reshape(tok_rows, flat_width),
    )


def solution(mesh):
    placed = (
        P("seq", "head"),
        P("seq", "head"),
        P("seq", "head"),
        P("seq", "head"),
        P("head", None),
        P("seq", "head"),
    )
    return jax.shard_map(
        local,
        mesh=mesh,
        in_specs=placed,
        out_specs=(P("seq", "head"), P("seq", "head"), P("seq", "head"), P("seq", "head")),
        check_vma=False,
    )
```

profile of v0, /device:TPU:0, one launch (start us, length us, event | category | flops | bytes accessed | tf_op | source)
XLA Modules:
  0.0 168.2 jit_solution(11531859500850806780)
XLA Ops:
  8.3 2.2 %fusion.16 = f32[8,128,128]{2,1,0:T(8,128)} fusion(f32[128,8]{0,1:T(8,128)S(1)} %copy.70, bf16[128,1024]{1,0:T(8,128)(2,1)S(1)} %copy-done, bf16[128,1024]{1,0:T(8,128)(2,1)} %param.11), kind=kOutput, calls=%fused_computation.37 | convolution fusion | flops 33947648 | bytes 1052672 | tf_op jit(solution)/shard_map/thd,the->hde/dot_general | solution.py:81
  10.7 1.1 copy.97
  11.8 10.3 %all_gather.26 = bf16[128,3072]{1,0:T(8,128)(2,1)S(1)} all-gather(bf16[128,768]{1,0:T(8,128)(2,1)} %param.15), channel_id=1, replica_groups=mesh['seq'=8,'head'=4] {'head'}, dimensions={1}, use_global_device_ids=true | all-gather | bytes 983040 | tf_op jit(solution)/shard_map/all_gather | solution.py:62
  22.1 5.1 %convolution_convert_fusion.2 = bf16[128,1024]{1,0:T(8,128)(2,1)S(1)} fusion(bf16[128,3072]{1,0:T(8,128)(2,1)S(1)} %all_gather.26, bf16[1024,3072]{1,0:T(8,128)(2,1)} %param.14), kind=kOutput, calls=%fused_computation.24 | convolution fusion | flops 805437440 | bytes 7340032 | tf_op jit(solution)/shard_map/dot_general | solution.py:61
  30.0 21.2 %all-gather.2 = f32[8,1,8]{2,1,0:T(1,128)S(1)} all-gather(f32[1,1,8]{2,1,0:T(1,128)S(1)} %get-tuple-element.302), channel_id=1, replica_groups=mesh['seq'=8,'head'=4] {'seq'}, dimensions={0}, use_global_device_ids=true | all-gather | bytes 288 | tf_op jit(solution)/shard_map/all_gather | solution.py:9
  51.4 17.2 %all-gather.3 = bf16[8,1,8]{2,1,0:T(2,128)(2,1)S(1)} all-gather(bf16[1,1,8]{2,1,0:T(2,128)(2,1)S(1)} %get-tuple-element.300), channel_id=1, replica_groups=mesh['seq'=8,'head'=4] {'seq'}, dimensions={0}, use_global_device_ids=true | all-gather | bytes 144 | tf_op jit(solution)/shard_map/all_gather | solution.py:24
  68.5 1.2 fusion.35
  69.7 16.6 %all-gather.7.cloned.1.call-done = f32[64,128,128]{2,1,0:T(8,128)} async-done(((f32[8,128,128]{2,1,0:T(8,128)}), f32[64,128,128]{2,1,0:T(8,128)}) %all-gather.7.cloned.1.call-update) | async-done | bytes 4194320 | tf_op jit(solution)/shard_map/all_gather | solution.py:9
  86.3 8.5 %while.30 = (s32[]{:T(128)}, f32[8,128,128]{2,1,0:T(8,128)S(1)}, s32[]{:T(128)}, f32[8,8]{1,0:T(8,128)S(1)}, f32[8,8,128,128]{3,2,1,0:T(8,128)}, /*index=5*/s32[]{:T(128)}, s32[]{:T(128)}) while((s32[]{:T(128)}, f32[8,128,128]{2,1,0:T(8,128)S(1)}, s32[]{:T(128)}, f32[8,8]{1,0:T(8,128)S(1)}, f32[8,8,128,128]{3,2,1,0:T(8,128)}, ...), condition=%wide.region_2.3_spmd.clone, body=%wide.region_1.2_spmd.clone.sunk | while | flops 524292 | bytes 1573073 | solution.py:18
  86.4 1.2 fusion.59
  87.6 1.2 fusion.59
  88.8 1.2 fusion.59
  90.0 1.2 fusion.59
  91.2 1.2 fusion.59
  92.4 1.2 fusion.59
  93.6 1.2 fusion.59
  95.1 1.3 fusion.12
  96.4 4.7 %convolution_convert_fusion = bf16[128,3072]{1,0:T(8,128)(2,1)} fusion(bf16[128,1024]{0,1:T(8,128)(2,1)S(1)} %bitcast.131, bf16[1024,3072]{1,0:T(8,128)(2,1)} %param.14), kind=kOutput, calls=%fused_computation.6 | convolution fusion | flops 805699584 | bytes 7340032 | tf_op jit(solution)/shard_map/dot_general | solution.py:115
  101.2 35.6 %all-gather.9.cloned.1.call-done = bf16[64,128,128]{2,1,0:T(8,128)(2,1)} async-done(((bf16[8,128,128]{2,1,0:T(8,128)(2,1)}), bf16[64,128,128]{2,1,0:T(8,128)(2,1)}) %all-gather.9.cloned.1.call-update) | async-done | bytes 2097168 | tf_op jit(solution)/shard_map/all_gather | solution.py:24
  136.7 9.1 %while.31 = (s32[]{:T(128)}, f32[8,128,128]{2,1,0:T(8,128)S(1)}, s32[]{:T(128)}, bf16[8,8]{1,0:T(8,128)(2,1)S(1)}, bf16[8,8,128,128]{3,2,1,0:T(8,128)(2,1)}, /*index=5*/s32[]{:T(128)}, s32[]{:T(128)}, s32[]{:T(128)}, s32[]{:T(128)}) while((s32[]{:T(128)}, f32[8,128,128]{2,1,0:T(8,128)S(1)}, s32[]{:T(128)}, ...), condition=%wide.region_5.6_spmd.clone, body=%wide.region_4.5_spmd.clone.sunk | while | flops 655376 | bytes 1310975 | solution.py:42
  142.4 1.1 fusion.60
  143.6 1.1 fusion.60
  144.7 1.1 fusion.60
  149.8 11.9 %reduce-scatter.2.cloned.1.call-done = bf16[128,768]{1,0:T(8,128)(2,1)} async-done(((bf16[128,3072]{1,0:T(8,128)(2,1)}), bf16[128,768]{1,0:T(8,128)(2,1)}) %reduce-scatter.2.cloned.1.call-update) | async-done | bytes 196624 | tf_op jit(solution)/shard_map/reduce_scatter | solution.py:116
  (55 shorter events, 13.9 us)
Async XLA Ops:
  7.2 1.2 copy-start
  7.2 79.2 %all-gather.7.cloned.1.call-start = ((), (), s32[]{:S(2)}) async-start(), calls=%async_computation.2 | async-start | bytes 4718592 | tf_op jit(solution)/shard_map/all_gather | solution.py:9
  8.1 20.5 %copy-start.1 = (bf16[128,1024]{1,0:T(8,128)(2,1)S(1)}, bf16[128,1024]{1,0:T(8,128)(2,1)}, u32[]{:S(2)}) copy-start(bf16[128,1024]{1,0:T(8,128)(2,1)} %param.11) | copy-start | bytes 786436
  10.6 126.1 %all-gather.9.cloned.1.call-start = ((), (), s32[]{:S(2)}) async-start(), calls=%async_computation.3 | async-start | bytes 2359296 | tf_op jit(solution)/shard_map/all_gather | solution.py:24
  28.4 133.2 %reduce-scatter.2.cloned.1.call-start = ((), (), s32[]{:S(2)}) async-start(), calls=%async_computation.1 | async-start | bytes 983040 | tf_op jit(solution)/shard_map/reduce_scatter | solution.py:116
Sparse Core Ops, SparseCore 0:
  10.7 75.5 all-gather.6
  89.0 47.6 all-gather.8
  139.8 21.7 reduce-scatter.1
where the time goes:
time: 169 us; the launch traced here: 168 us
  waiting for transfers between devices  64.1 us (38%)
  blocking collectives  48.7 us (29%)
  matrix products  18.7 us (11%)
  other arithmetic  18 us (11%)
  between operations  13.9 us (8%)
  local copies, waits for them, and re-layouts  4.15 us (2%)
    all_gather x1, waiting for transfers between devices, entering(): lax.all_gather(part.astype(kind), axis)  35.6 us
    all_gather x1, blocking collectives, prefix(): pieces = jax.tree.map(lambda part: lax.all_gather(part, axis), value)  21.2 us
    all_gather x1, blocking collectives, entering(): lax.all_gather(part.astype(kind), axis)  17.2 us
    all_gather x1, waiting for transfers between devices, prefix(): pieces = jax.tree.map(lambda part: lax.all_gather(part, axis), value)  16.6 us
    reduce_scatter x1, waiting for transfers between devices, local(): lax.psum_scatter(partial_out.astype(jnp.bfloat16), 'head', scatter_dimens...  11.9 us
    all_gather x1, blocking collectives, local(): lax.all_gather(out_grad, 'head', axis=1, tiled=True)  10.3 us
    select_n x8, other arithmetic, entering_step(): return jax.tree.map(lambda a, b: jnp.where(reached, a, b), new, before)  8.77 us
    select_n x7, other arithmetic, prefix_step(): jnp.where(position < mine, new, old)  8.22 us
  transfers between devices with their start and end apart: 3, of which 3 were waited for; matrix products, arithmetic and copies ran while one was open for 22% of the time, Pallas kernels for 0%

commit v1 on v0

--- a/solution.py
+++ b/solution.py
@@ -2,6 +2,11 @@
 import jax.numpy as jnp
 from jax import lax
 from jax.sharding import PartitionSpec as P
+
+
+def gather_from_all(value, axis, dim):
+    copies = jnp.concatenate([value] * lax.axis_size(axis), axis=dim)
+    return lax.all_to_all(copies, axis, dim, dim, tiled=True)
 
 
 def prefix(value, axis, join, neutral):
@@ -59,7 +64,7 @@
     head_width = queries.shape[1] // head_count
     att_scale = 1.0 / head_width
     grad_flat = lax.dot_general(
-        lax.all_gather(out_grad, "head", axis=1, tiled=True),
+        gather_from_all(out_grad, "head", 1),
         out_weight,
         (((1,), (1,)), ((), ())),
         preferred_element_type=jnp.float32,

time: 169 us -> 169 us (level)
  blocking collectives: 48.7 us -> 38.4 us
  waiting for transfers between devices: 64.1 us -> 71 us
  starting transfers between devices: 0.12 us -> 4.35 us
  matrix products: 18.7 us -> 16.8 us
    all_gather x1 -> x0, blocking collectives: 10.3 us -> none  [local(): lax.all_gather(out_grad, 'head', axis=1, tiled=True)]
    all_gather x1, waiting for transfers between devices: 16.6 us -> 22.7 us  [prefix(): pieces = jax.tree.map(lambda part: lax.all_gather(part, axis), value)]
    all_gather x1, blocking collectives: 17.2 us -> 21.9 us  [entering(): lax.all_gather(part.astype(kind), axis)]
    all_gather x1, blocking collectives: 21.2 us -> 16.5 us  [prefix(): pieces = jax.tree.map(lambda part: lax.all_gather(part, axis), value)]
    all_to_all x0 -> x1, starting transfers between devices: none -> 4.26 us  [gather_from_all(): return lax.all_to_all(copies, axis, dim, dim, tiled=True)]
  transfers between devices with their start and end apart: 3 -> 4, of which waited for: 3 -> 3; matrix products, arithmetic and copies ran while one was open for 22% -> 22% of each run, Pallas kernels for 0% -> 0%
where the time goes in v1:
time: 169 us; the launch traced here: 168 us
  waiting for transfers between devices  71 us (42%)
  blocking collectives  38.4 us (23%)
  other arithmetic  18.1 us (11%)
  matrix products  16.8 us (10%)
  between operations  13.9 us (8%)
  local copies, waits for them, and re-layouts  4.96 us (3%)
  starting transfers between devices  4.35 us (3%)
    all_gather x1, waiting for transfers between devices, entering(): lax.all_gather(part.astype(kind), axis)  36.4 us
    all_gather x1, waiting for transfers between devices, prefix(): pieces = jax.tree.map(lambda part: lax.all_gather(part, axis), value)  22.7 us
    all_gather x1, blocking collectives, entering(): lax.all_gather(part.astype(kind), axis)  21.9 us
    all_gather x1, blocking collectives, prefix(): pieces = jax.tree.map(lambda part: lax.all_gather(part, axis), value)  16.5 us
    reduce_scatter x1, waiting for transfers between devices, local(): lax.psum_scatter(partial_out.astype(jnp.bfloat16), 'head', scatter_dimens...  11.8 us
    select_n x8, other arithmetic, entering_step(): return jax.tree.map(lambda a, b: jnp.where(reached, a, b), new, before)  8.77 us
    select_n x7, other arithmetic, prefix_step(): jnp.where(position < mine, new, old)  8.22 us
    dot_general x1, matrix products, local(): lax.dot_general(gather_from_all(out_grad, 'head', 1), out_weight, (((1,),...  5.03 us
  transfers between devices with their start and end apart: 4, of which 3 were waited for; matrix products, arithmetic and copies ran while one was open for 22% of the time, Pallas kernels for 0%

profile of v1, /device:TPU:0, one launch (start us, length us, event | category | flops | bytes accessed | tf_op | source)
XLA Modules:
  0.0 168.1 jit_solution(6873466792300278797)
XLA Ops:
  8.3 2.2 %fusion.16 = f32[8,128,128]{2,1,0:T(8,128)} fusion(f32[128,8]{0,1:T(8,128)S(1)} %copy.97, bf16[128,1024]{1,0:T(8,128)(2,1)S(1)} %copy-done, bf16[128,1024]{1,0:T(8,128)(2,1)} %param.11), kind=kOutput, calls=%fused_computation.38 | convolution fusion | flops 33947648 | bytes 1052672 | tf_op jit(solution)/shard_map/thd,the->hde/dot_general | solution.py:86
  10.9 1.2 copy.109
  12.0 4.3 %all-to-all-start = ((bf16[128,4,768]{2,0,1:T(8,128)(2,1)}), bf16[128,4,768]{2,0,1:T(8,128)(2,1)S(1)}, u32[]{:S(2)}, u32[]{:S(2)}) async-start(bf16[128,4,768]{2,0,1:T(8,128)(2,1)} %copy.109), calls=%async_computation.1 | async-start | bytes 1572864 | tf_op jit(solution)/shard_map/all_to_all | solution.py:9
  16.6 21.9 %all-gather.3 = bf16[8,1,8]{2,1,0:T(2,128)(2,1)S(1)} all-gather(bf16[1,1,8]{2,1,0:T(2,128)(2,1)S(1)} %get-tuple-element.304), channel_id=1, replica_groups=mesh['seq'=8,'head'=4] {'seq'}, dimensions={0}, use_global_device_ids=true | all-gather | bytes 144 | tf_op jit(solution)/shard_map/all_gather | solution.py:29
  38.5 16.5 %all-gather.2 = f32[8,1,8]{2,1,0:T(1,128)S(1)} all-gather(f32[1,1,8]{2,1,0:T(1,128)S(1)} %get-tuple-element.306), channel_id=1, replica_groups=mesh['seq'=8,'head'=4] {'seq'}, dimensions={0}, use_global_device_ids=true | all-gather | bytes 288 | tf_op jit(solution)/shard_map/all_gather | solution.py:14
  56.5 5.0 %convolution_convert_fusion.2 = bf16[128,1024]{1,0:T(8,128)(2,1)S(1)} fusion(bf16[128,3072]{0,1:T(8,128)(2,1)S(1)} %bitcast.133, bf16[1024,3072]{1,0:T(8,128)(2,1)} %param.14), kind=kOutput, calls=%fused_computation.24 | convolution fusion | flops 805437440 | bytes 7340032 | tf_op jit(solution)/shard_map/dot_general | solution.py:66
  63.6 22.7 %all-gather.7.cloned.1.call-done = f32[64,128,128]{2,1,0:T(8,128)} async-done(((f32[8,128,128]{2,1,0:T(8,128)}), f32[64,128,128]{2,1,0:T(8,128)}) %all-gather.7.cloned.1.call-update) | async-done | bytes 4194320 | tf_op jit(solution)/shard_map/all_gather | solution.py:14
  86.3 8.5 %while.30 = (s32[]{:T(128)}, f32[8,128,128]{2,1,0:T(8,128)S(1)}, s32[]{:T(128)}, f32[8,8]{1,0:T(8,128)S(1)}, f32[8,8,128,128]{3,2,1,0:T(8,128)}, /*index=5*/s32[]{:T(128)}, s32[]{:T(128)}) while((s32[]{:T(128)}, f32[8,128,128]{2,1,0:T(8,128)S(1)}, s32[]{:T(128)}, f32[8,8]{1,0:T(8,128)S(1)}, f32[8,8,128,128]{3,2,1,0:T(8,128)}, ...), condition=%wide.region_2.3_spmd.clone, body=%wide.region_1.2_spmd.clone.sunk | while | flops 524292 | bytes 1573073 | solution.py:23
  86.3 1.2 fusion.59
  87.5 1.2 fusion.59
  88.8 1.2 fusion.59
  90.0 1.2 fusion.59
  91.2 1.2 fusion.59
  92.4 1.2 fusion.59
  93.6 1.2 fusion.59
  95.4 4.8 %convolution_convert_fusion = bf16[128,3072]{1,0:T(8,128)(2,1)} fusion(bf16[128,1024]{0,1:T(8,128)(2,1)S(1)} %bitcast.135, bf16[1024,3072]{1,0:T(8,128)(2,1)} %param.14), kind=kOutput, calls=%fused_computation.6 | convolution fusion | flops 805699584 | bytes 7340032 | tf_op jit(solution)/shard_map/dot_general | solution.py:120
  100.3 36.4 %all-gather.9.cloned.1.call-done = bf16[64,128,128]{2,1,0:T(8,128)(2,1)} async-done(((bf16[8,128,128]{2,1,0:T(8,128)(2,1)}), bf16[64,128,128]{2,1,0:T(8,128)(2,1)}) %all-gather.9.cloned.1.call-update) | async-done | bytes 2097168 | tf_op jit(solution)/shard_map/all_gather | solution.py:29
  136.7 9.1 %while.31 = (s32[]{:T(128)}, f32[8,128,128]{2,1,0:T(8,128)S(1)}, s32[]{:T(128)}, bf16[8,8]{1,0:T(8,128)(2,1)S(1)}, bf16[8,8,128,128]{3,2,1,0:T(8,128)(2,1)}, /*index=5*/s32[]{:T(128)}, s32[]{:T(128)}, s32[]{:T(128)}, s32[]{:T(128)}) while((s32[]{:T(128)}, f32[8,128,128]{2,1,0:T(8,128)S(1)}, s32[]{:T(128)}, ...), condition=%wide.region_5.6_spmd.clone, body=%wide.region_4.5_spmd.clone.sunk | while | flops 655376 | bytes 1310975 | solution.py:47
  137.8 1.1 fusion.60
  139.0 1.1 fusion.60
  142.4 1.1 fusion.60
  143.5 1.1 fusion.60
  144.7 1.1 fusion.60
  149.8 11.8 %reduce-scatter.2.cloned.1.call-done = bf16[128,768]{1,0:T(8,128)(2,1)} async-done(((bf16[128,3072]{1,0:T(8,128)(2,1)}), bf16[128,768]{1,0:T(8,128)(2,1)}) %reduce-scatter.2.cloned.1.call-update) | async-done | bytes 196624 | tf_op jit(solution)/shard_map/reduce_scatter | solution.py:121
  (68 shorter events, 13.1 us)
Async XLA Ops:
  7.2 1.2 copy-start
  7.2 3.4 %copy-start.5 = (bf16[128,768]{1,0:T(8,128)(2,1)S(1)}, bf16[128,768]{1,0:T(8,128)(2,1)}, u32[]{:S(2)}) copy-start(bf16[128,768]{1,0:T(8,128)(2,1)} %param.15) | copy-start | bytes 589828
  7.2 79.1 %all-gather.7.cloned.1.call-start = ((), (), s32[]{:S(2)}) async-start(), calls=%async_computation.3 | async-start | bytes 4718592 | tf_op jit(solution)/shard_map/all_gather | solution.py:14
  10.8 5.5 %copy-start.4 = (bf16[128,1024]{1,0:T(8,128)(2,1)S(1)}, bf16[128,1024]{1,0:T(8,128)(2,1)}, u32[]{:S(2)}) copy-start(bf16[128,1024]{1,0:T(8,128)(2,1)} %param.10) | copy-start | bytes 786436
  10.8 44.2 %copy-start.1 = (bf16[128,1024]{1,0:T(8,128)(2,1)S(1)}, bf16[128,1024]{1,0:T(8,128)(2,1)}, u32[]{:S(2)}) copy-start(bf16[128,1024]{1,0:T(8,128)(2,1)} %param.11) | copy-start | bytes 786436
  12.0 44.1 %all-to-all-start = ((bf16[128,4,768]{2,0,1:T(8,128)(2,1)}), bf16[128,4,768]{2,0,1:T(8,128)(2,1)S(1)}, u32[]{:S(2)}, u32[]{:S(2)}) async-start(bf16[128,4,768]{2,0,1:T(8,128)(2,1)} %copy.109), calls=%async_computation.1 | async-start | bytes 1572864 | tf_op jit(solution)/shard_map/all_to_all | solution.py:9
  16.3 120.4 %all-gather.9.cloned.1.call-start = ((), (), s32[]{:S(2)}) async-start(), calls=%async_computation.4 | async-start | bytes 2359296 | tf_op jit(solution)/shard_map/all_gather | solution.py:29
  61.5 1.8 %copy-start.3 = (bf16[8,128,128]{2,1,0:T(8,128)(2,1)S(1)}, bf16[8,128,128]{2,1,0:T(8,128)(2,1)}, u32[]{:S(2)}) copy-start(bf16[8,128,128]{2,1,0:T(8,128)(2,1)} %fusion.7) | copy-start | bytes 786436
  63.3 98.3 %reduce-scatter.2.cloned.1.call-start = ((), (), s32[]{:S(2)}) async-start(), calls=%async_computation.2 | async-start | bytes 983040 | tf_op jit(solution)/shard_map/reduce_scatter | solution.py:121
  145.8 1.2 copy-start.2
Sparse Core Ops, SparseCore 0:
  10.7 75.5 all-gather.6
  89.0 47.6 all-gather.8
  139.8 21.7 reduce-scatter.1
